TPU v7x, 512 devices: a whole 4x8x8 slice. The times are simulated.
512 devices in a mesh: row: 32 (over y_lo, x, core), col: 16 (over z, y_hi).
Axes of the slice: x: 4, y: 8 (y_hi: 2, y_lo: 4; y = y_hi * 4 + y_lo), z: 8, core: 2. Of those that a mesh axis runs over, the one named last changes fastest.
Arguments:
- vorticity_coefficients: bfloat16 [3, 512, 512, 512], P(None, 'row', 'col'), may hold values from -6 to 6
Outputs:
- enstrophy: float32 [512, 512, 512], P('row', 'col')
- normals: bfloat16 [3, 512, 512, 512], P(None, 'row', 'col')
All inputs are finite; a program needn't handle non-finite values.
Results may differ from a plain program's by a relative error of at most 0.001.
Values sent between devices are 32-bit elements; how exact they have to be, the bound alone decides.
A program may use at most 64 MiB of HBM per device.

v0:
```python
import functools

import jax
import jax.numpy as jnp
import numpy as np
from jax import lax
from jax.experimental import pallas as pl
from jax.experimental.pallas import tpu as pltpu
from jax.sharding import PartitionSpec as P

MESH = pl.DeviceIdType.MESH
NT = (((1,), (1,)), ((), ()))
ORDER = (4, 3, 5, 2, 6, 1, 7)


def fourier_table(n):
    k = np.arange(n)[:, None]
    x = np.arange(n)[None, :]
    h = n // 2
    f = np.where(k <= h, k, k - h)
    angle = (f * x % n) * (2.0 * np.pi / n)
    weight = np.where((k == 0) | (k == h), np.sqrt(1.0 / n), np.sqrt(2.0 / n))
    return (np.where(k <= h, np.cos(angle), np.sin(angle)) * weight).astype(np.float32)


def split(table):
    high = table.astype(jnp.bfloat16)
    low = (table - high.astype(np.float32)).astype(jnp.bfloat16)
    return high, low


def tables(n):
    t = fourier_table(n)
    p, xc, i = np.meshgrid(np.arange(8), np.arange(8), np.arange(8), indexing="ij")
    x_order = (((p % 4) * 8 + xc) * 16 + (p // 4) * 8 + i).reshape(-1)
    bi, g = np.meshgrid(np.arange(16), np.arange(32), indexing="ij")
    b_order = (g * 16 + bi).reshape(-1)
    yh, zs, qj = np.meshgrid(np.arange(2), np.arange(8), np.arange(32), indexing="ij")
    q_order = ((zs * 2 + yh) * 32 + qj).reshape(-1)
    first = split(np.ascontiguousarray(t[:, x_order].T))
    second = split(np.ascontiguousarray(t[b_order].T))
    third = split(np.ascontiguousarray(t[q_order]))
    return first + second + third


def swap_groups(parts):
    lane = lax.broadcasted_iota(jnp.int32, parts[0].shape, 1)
    low_half = lane < 64
    even = (lane // 32) % 2 == 0
    p0, p1, p2, p3 = parts
    a0 = jnp.where(low_half, p0, pltpu.roll(p2, 64, 1))
    a2 = jnp.where(low_half, pltpu.roll(p0, 64, 1), p2)
    a1 = jnp.where(low_half, p1, pltpu.roll(p3, 64, 1))
    a3 = jnp.where(low_half, pltpu.roll(p1, 64, 1), p3)
    out = []
    for u, v in ((a0, a1), (a2, a3)):
        out.append(jnp.where(even, u, pltpu.roll(v, 32, 1)))
        out.append(jnp.where(even, pltpu.roll(u, 96, 1), v))
    return out


def kernel(
    x_ref, t1h, t1l, t2h, t2l, t3h, t3l, e_ref, n_ref,
    out1, r1, a, bh, bl, out2, cc, ch, cl, acc, ext, edge, halo,
    send, y_sem, x_sem, z_sem, e_sem, h_sem,
):
    row = lax.axis_index("row")
    col = lax.axis_index("col")
    y_lo, xc = row // 8, row % 8
    z, y_hi = col // 2, col % 2
    y = y_hi * 4 + y_lo

    def at_y(d):
        t = (y + d) % 8
        return t, {"row": (t % 4) * 8 + xc, "col": z * 2 + t // 4}

    def at_x(d):
        t = (xc + d) % 8
        return t, {"row": y_lo * 8 + t, "col": col}

    def at_z(d):
        t = (z + d) % 8
        return t, {"row": row, "col": t * 2 + y_hi}

    partner = at_y(4)[1]
    up = {"row": (row + 1) % 32, "col": col}
    down = {"row": (row + 31) % 32, "col": col}
    right = {"row": row, "col": (col + 1) % 16}
    left = {"row": row, "col": (col + 15) % 16}

    barrier = pltpu.get_barrier_semaphore()
    for d in ORDER:
        for at in (at_y, at_x, at_z):
            pl.semaphore_signal(barrier, inc=1, device_id=at(d)[1], device_id_type=MESH)
    for who in (up, down, right, left):
        pl.semaphore_signal(barrier, inc=1, device_id=who, device_id_type=MESH)

    def first(c):
        for n in range(2):
            data = x_ref[c, n * 256 : (n + 1) * 256, :]
            for m in range(2):
                rows = slice(m * 256, (m + 1) * 256)
                got = lax.dot_general(t1h[rows, :], data, NT, preferred_element_type=jnp.float32)
                got += lax.dot_general(t1l[rows, :], data, NT, preferred_element_type=jnp.float32)
                for h in range(2):
                    out1[c, n * 2 + h, m * 4 : (m + 1) * 4] = got[:, h * 128 : (h + 1) * 128].reshape(4, 64, 128)

    def remote(src, dst, s, r, who):
        pltpu.make_async_remote_copy(
            src_ref=src, dst_ref=dst, send_sem=s, recv_sem=r, device_id=who, device_id_type=MESH
        ).start()

    def send_y(c):
        for d in ORDER:
            t, who = at_y(d)
            remote(out1.at[c, :, t], r1.at[c, :, y], send.at[0], y_sem.at[c], who)
        r1[c, :, y] = out1[c, :, y]

    def wait(ref, sem):
        pltpu.make_async_copy(ref, ref, sem).wait()

    first(0)
    pl.semaphore_wait(barrier, 25)
    send_y(0)
    first(1)
    send_y(1)
    first(2)
    send_y(2)

    def gather_x(c):
        wait(r1.at[c, :, pl.ds(0, 7)], y_sem.at[c])
        for d in ORDER:
            t, who = at_x(d)
            remote(
                r1.at[c, :, :, pl.ds(pl.multiple_of(t * 8, 8), 8), :],
                a.at[c, :, :, pl.ds(pl.multiple_of(xc * 8, 8), 8), :],
                send.at[1], x_sem.at[c], who,
            )
        own = pl.ds(pl.multiple_of(xc * 8, 8), 8)
        a[c, :, :, own, :] = r1[c, :, :, own, :]
        wait(a.at[c, :, pl.ds(0, 7)], x_sem.at[c])

    def second(c):
        def tile(t, carry):
            for half in range(2):
                for quad in range(2):
                    for pair in range(2):
                        parts = []
                        for i in range(4):
                            rows = pl.ds(quad * 4 + i, 8, stride=8)
                            s = half * 4 + pair * 2
                            parts.append(jnp.concatenate([a[c, t, s, rows, :], a[c, t, s + 1, rows, :]], axis=0))
                        lanes = slice((half * 2 + quad) * 128, (half * 2 + quad + 1) * 128)
                        for j, part in enumerate(swap_groups(parts)):
                            high = part.astype(jnp.bfloat16)
                            low = (part - high.astype(jnp.float32)).astype(jnp.bfloat16)
                            rows = pl.ds(pl.multiple_of(t * 128 + (j * 32 + pair * 16), 16), 16)
                            bh[rows, lanes] = high
                            bl[rows, lanes] = low
            return carry

        lax.fori_loop(0, 4, tile, 0)
        for m in range(2):
            rows = slice(m * 256, (m + 1) * 256)
            got = jnp.dot(t2h[rows, :], bh[...], preferred_element_type=jnp.float32)
            got += jnp.dot(t2l[rows, :], bh[...], preferred_element_type=jnp.float32)
            got += jnp.dot(t2h[rows, :], bl[...], preferred_element_type=jnp.float32)
            out2[c, m * 4 : (m + 1) * 4] = got.reshape(4, 64, 512)
        for d in ORDER:
            t, who = at_z(d)
            remote(out2.at[c, t], cc.at[c, z], send.at[2], z_sem.at[c], who)
        cc[c, z] = out2[c, z]

    def third(c, after):
        wait(cc.at[c, pl.ds(0, 7)], z_sem.at[c])
        for quad in range(2):
            for half in range(2):
                for zq in range(2):
                    lanes = slice((half * 2 + quad) * 128, (half * 2 + quad + 1) * 128)
                    into = slice((half * 2 + zq) * 128, (half * 2 + zq + 1) * 128)
                    parts = [cc[c, zq * 4 + k, :, lanes] for k in range(4)]
                    for i, part in enumerate(swap_groups(parts)):
                        high = part.astype(jnp.bfloat16)
                        rows = slice((quad * 4 + i) * 64, (quad * 4 + i + 1) * 64)
                        ch[rows, into] = high
                        cl[rows, into] = (part - high.astype(jnp.float32)).astype(jnp.bfloat16)
            rows = slice(quad * 256, (quad + 1) * 256)
            got = jnp.dot(ch[rows, :], t3h[...], preferred_element_type=jnp.float32)
            got += jnp.dot(cl[rows, :], t3h[...], preferred_element_type=jnp.float32)
            got += jnp.dot(ch[rows, :], t3l[...], preferred_element_type=jnp.float32)
            level = (0.5 * got * got).reshape(4, 64, 512)
            planes = slice(quad * 4, (quad + 1) * 4)
            acc[planes] = jnp.where(c == 0, level, acc[planes] + level)
            after(quad)

    def step(c, carry):
        gather_x(c)
        second(c)

        @pl.when(c > 0)
        def _():
            third(c - 1, lambda quad: None)

        return carry

    lax.fori_loop(0, 3, step, 0)

    mine = pl.ds(pl.multiple_of(y_hi * 32, 32), 32)
    theirs = pl.ds(pl.multiple_of((1 - y_hi) * 32, 32), 32)

    def exchange(quad):
        planes = pl.ds(quad * 4, 4)
        slot = pl.ds(1 + y_hi * 8 + quad * 4, 4)
        remote(acc.at[planes, theirs, :], ext.at[slot], send.at[3], e_sem.at[0], partner)
        ext[slot] = acc[planes, mine, :]

    third(2, exchange)
    wait(acc.at[:, pl.ds(0, 32), :], e_sem.at[0])

    remote(ext.at[16], ext.at[0], send.at[4], h_sem.at[0], up)
    remote(ext.at[1], ext.at[17], send.at[5], h_sem.at[1], down)
    edge[0] = ext[1:17, 31, :]
    edge[1] = ext[1:17, 0, :]
    remote(edge.at[0], halo.at[0], send.at[6], h_sem.at[2], right)
    remote(edge.at[1], halo.at[1], send.at[7], h_sem.at[3], left)
    e_ref[...] = ext[1:17]
    wait(ext.at[0], h_sem.at[0])
    wait(ext.at[17], h_sem.at[1])
    wait(halo.at[0], h_sem.at[2])
    wait(halo.at[1], h_sem.at[3])

    place = lax.broadcasted_iota(jnp.int32, (32, 512), 0)

    def plane(i, carry):
        centre = ext[i + 1]
        step_x = 0.5 * (ext[i + 2] - ext[i])
        after = jnp.where(place == 31, halo[1, pl.ds(i, 1), :], pltpu.roll(centre, 31, 0))
        before = jnp.where(place == 0, halo[0, pl.ds(i, 1), :], pltpu.roll(centre, 1, 0))
        step_y = 0.5 * (after - before)
        step_z = 0.5 * (pltpu.roll(centre, 511, 1) - pltpu.roll(centre, 1, 1))
        square = step_x * step_x + step_y * step_y + step_z * step_z
        scale = -lax.rsqrt(jnp.maximum(square, 1.0))
        n_ref[0, i] = (step_x * scale).astype(jnp.bfloat16)
        n_ref[1, i] = (step_y * scale).astype(jnp.bfloat16)
        n_ref[2, i] = (step_z * scale).astype(jnp.bfloat16)
        return carry

    lax.fori_loop(0, 16, plane, 0)

    wait(out1.at[:, :, pl.ds(0, 7)], send.at[0])
    wait(a.at[:, :, pl.ds(0, 7)], send.at[1])
    wait(out2.at[:, pl.ds(0, 7)], send.at[2])
    wait(acc.at[:, pl.ds(0, 32), :], send.at[3])
    wait(ext.at[16], send.at[4])
    wait(ext.at[1], send.at[5])
    wait(edge.at[0], send.at[6])
    wait(edge.at[1], send.at[7])


def body(coefficients):
    members, span_b, span_q, length = coefficients.shape
    data = coefficients.reshape(members, span_b * span_q, length)
    whole = pl.BlockSpec(memory_space=pltpu.VMEM)
    f32, bf16 = jnp.float32, jnp.bfloat16
    return pl.pallas_call(
        kernel,
        out_shape=(
            jax.ShapeDtypeStruct((16, 32, 512), f32),
            jax.ShapeDtypeStruct((3, 16, 32, 512), bf16),
        ),
        in_specs=[whole] * 7,
        out_specs=(whole, whole),
        scratch_shapes=[
            pltpu.VMEM((3, 4, 8, 64, 128), f32),
            pltpu.VMEM((3, 4, 8, 64, 128), f32),
            pltpu.VMEM((3, 4, 8, 64, 128), f32),
            pltpu.VMEM((512, 512), bf16),
            pltpu.VMEM((512, 512), bf16),
            pltpu.VMEM((3, 8, 64, 512), f32),
            pltpu.VMEM((3, 8, 64, 512), f32),
            pltpu.VMEM((512, 512), bf16),
            pltpu.VMEM((512, 512), bf16),
            pltpu.VMEM((8, 64, 512), f32),
            pltpu.VMEM((18, 32, 512), f32),
            pltpu.VMEM((2, 16, 512), f32),
            pltpu.VMEM((2, 16, 512), f32),
            pltpu.SemaphoreType.DMA((8,)),
            pltpu.SemaphoreType.DMA((3,)),
            pltpu.SemaphoreType.DMA((3,)),
            pltpu.SemaphoreType.DMA((3,)),
            pltpu.SemaphoreType.DMA((1,)),
            pltpu.SemaphoreType.DMA((4,)),
        ],
        compiler_params=pltpu.CompilerParams(
            collective_id=0, has_side_effects=True, vmem_limit_bytes=56 * 1024 * 1024
        ),
        name="vorticity_normals",
    )(data, *tables(length))


def solution(mesh):
    return jax.shard_map(
        body,
        mesh=mesh,
        in_specs=(P(None, "row", "col", None),),
        out_specs=(P("row", "col", None), P(None, "row", "col", None)),
        check_vma=False,
    )
```

profile of v0, /device:TPU:1, one launch (start us, length us, event | category | flops | bytes accessed | tf_op | source)
XLA Modules:
  0.0 169.6 jit_solution(8292803644590096908)
XLA Ops:
  0.6 165.4 %vorticity_normals.1 = (f32[16,32,512]{2,1,0:T(8,128)}, bf16[3,16,32,512]{3,2,1,0:T(8,128)(2,1)}) custom-call(bf16[3,512,512]{2,1,0:T(8,128)(2,1)} %bitcast.1, bf16[512,512]{1,0:T(8,128)(2,1)} %constant.12.clone.t1h, bf16[512,512]{1,0:T(8,128)(2,1)} %constant.13.clone.t1l, bf16[512,512]{1,0:T(8,128)(2,1)} %constant.14.clone.t2h, ...), custom_call_target="tpu_custom_call" | custom-call | tf_op jit(solution)/shard_map/vorticity_normals/pallas_call | solution.py:265
  166.0 0.0 copy-start
  166.1 2.4 %copy.11 = f32[16,32,512]{2,1,0:T(8,128)} copy(f32[16,32,512]{2,1,0:T(8,128)} %get-tuple-element.4) | data formatting | bytes 2097152
  168.5 0.0 copy-done
  168.5 1.1 copy.12
Async XLA Ops:
  166.0 2.4 %copy-start = (bf16[3,16,32,512]{3,2,1,0:T(8,128)(2,1)S(1)}, bf16[3,16,32,512]{3,2,1,0:T(8,128)(2,1)}, u32[]{:S(2)}) copy-start(bf16[3,16,32,512]{3,2,1,0:T(8,128)(2,1)} %get-tuple-element.5) | copy-start | bytes 4718596
where the time goes:
time: 170 us
  Pallas kernels  165 us (97%)
  local copies, waits for them, and re-layouts  3.55 us (2%)
    pallas_call x1, Pallas kernels, body(): pl.pallas_call(kernel, out_shape=(jax.ShapeDtypeStruct((16, 32, 512), f32...  165 us
    unnamed x4, local copies, waits for them, and re-layouts  3.55 us

commit v1 on v0

v1 whole, which is shorter than its diff:
```python
import functools

import jax
import jax.numpy as jnp
import numpy as np
from jax import lax
from jax.experimental import pallas as pl
from jax.experimental.pallas import tpu as pltpu
from jax.sharding import PartitionSpec as P

MESH = pl.DeviceIdType.MESH
NT = (((1,), (1,)), ((), ()))
VMEM_MIB = 40
ORDER = (4, 3, 5, 2, 6, 1, 7)


def fourier_table(n):
    k = np.arange(n)[:, None]
    x = np.arange(n)[None, :]
    h = n // 2
    f = np.where(k <= h, k, k - h)
    angle = (f * x % n) * (2.0 * np.pi / n)
    weight = np.where((k == 0) | (k == h), np.sqrt(1.0 / n), np.sqrt(2.0 / n))
    return (np.where(k <= h, np.cos(angle), np.sin(angle)) * weight).astype(np.float32)


def split(table):
    high = table.astype(jnp.bfloat16)
    low = (table - high.astype(np.float32)).astype(jnp.bfloat16)
    return high, low


def tables(n):
    t = fourier_table(n)
    p, xc, i = np.meshgrid(np.arange(8), np.arange(8), np.arange(8), indexing="ij")
    x_order = (((p % 4) * 8 + xc) * 16 + (p // 4) * 8 + i).reshape(-1)
    h, zs, j = np.meshgrid(np.arange(2), np.arange(8), np.arange(32), indexing="ij")
    y_order = (zs * 64 + h * 32 + j).reshape(-1)
    bi, g = np.meshgrid(np.arange(16), np.arange(32), indexing="ij")
    b_order = (g * 16 + bi).reshape(-1)
    yh, zs, qj = np.meshgrid(np.arange(2), np.arange(8), np.arange(32), indexing="ij")
    q_order = ((zs * 2 + yh) * 32 + qj).reshape(-1)
    first = split(np.ascontiguousarray(t[:, x_order].T))
    second = split(np.ascontiguousarray(t[b_order][:, y_order].T))
    third = split(np.ascontiguousarray(t[q_order]))
    return np.stack(first + second + third)


def swap_groups(parts):
    lane = lax.broadcasted_iota(jnp.int32, parts[0].shape, 1)
    low_half = lane < 64
    even = (lane // 32) % 2 == 0
    p0, p1, p2, p3 = parts
    a0 = jnp.where(low_half, p0, pltpu.roll(p2, 64, 1))
    a2 = jnp.where(low_half, pltpu.roll(p0, 64, 1), p2)
    a1 = jnp.where(low_half, p1, pltpu.roll(p3, 64, 1))
    a3 = jnp.where(low_half, pltpu.roll(p1, 64, 1), p3)
    out = []
    for u, v in ((a0, a1), (a2, a3)):
        out.append(jnp.where(even, u, pltpu.roll(v, 32, 1)))
        out.append(jnp.where(even, pltpu.roll(u, 96, 1), v))
    return out


def kernel(
    x_hbm, t_hbm, e_ref, n_ref,
    x_ref, tab, out1, r1, a, bh, bl, out2, cc, ch, cl, acc, ext, edge, halo, nrm,
    load, store, send, y_sem, x_sem, z_sem, e_sem, h_sem,
):
    row = lax.axis_index("row")
    col = lax.axis_index("col")
    y_lo, xc = row // 8, row % 8
    z, u = col // 2, col % 2
    y = u * 4 + y_lo

    def at_y(d):
        t = (y + d) % 8
        return t, {"row": (t % 4) * 8 + xc, "col": z * 2 + t // 4}

    def at_x(d):
        t = (xc + d) % 8
        return t, {"row": y_lo * 8 + t, "col": col}

    def at_z(d):
        t = (z + d) % 8
        return t, {"row": row, "col": t * 2 + u}

    partner = at_y(4)[1]
    up = {"row": (row + 1) % 32, "col": col}
    down = {"row": (row + 31) % 32, "col": col}
    beside = {"row": row, "col": (col + 15 + 2 * u) % 16}
    beyond = {"row": row, "col": (col + 2 + 12 * u) % 16}

    barrier = pltpu.get_barrier_semaphore()
    for d in ORDER:
        for at in (at_y, at_x, at_z):
            pl.semaphore_signal(barrier, inc=1, device_id=at(d)[1], device_id_type=MESH)
    for who in (up, down, beside):
        pl.semaphore_signal(barrier, inc=1, device_id=who, device_id_type=MESH)

    def wait(ref, sem):
        pltpu.make_async_copy(ref, ref, sem).wait()

    loads = [pltpu.make_async_copy(t_hbm.at[pl.ds(2 * i, 2)], tab.at[pl.ds(2 * i, 2)], load.at[i]) for i in range(3)]
    loads += [pltpu.make_async_copy(x_hbm.at[c], x_ref.at[c], load.at[3 + c]) for c in range(3)]
    for i in (0, 3, 4, 5, 1, 2):
        loads[i].start()

    def remote(src, dst, s, r, who):
        pltpu.make_async_remote_copy(
            src_ref=src, dst_ref=dst, send_sem=s, recv_sem=r, device_id=who, device_id_type=MESH
        ).start()

    def first(c, n):
        data = x_ref[c, n * 256 : (n + 1) * 256, :]
        for m in range(2):
            rows = slice(m * 256, (m + 1) * 256)
            got = lax.dot_general(tab[0, rows, :], data, NT, preferred_element_type=jnp.float32)
            got += lax.dot_general(tab[1, rows, :], data, NT, preferred_element_type=jnp.float32)
            for h in range(2):
                out1[c, n * 2 + h, m * 4 : (m + 1) * 4] = got[:, h * 128 : (h + 1) * 128].reshape(4, 64, 128)

    def send_y(c, n):
        two = pl.ds(n * 2, 2)
        for d in ORDER:
            t, who = at_y(d)
            remote(out1.at[c, two, t], r1.at[c, two, y], send.at[0], y_sem.at[c * 2 + n], who)
        r1[c, two, y] = out1[c, two, y]

    loads[0].wait()
    for c in range(3):
        loads[3 + c].wait()
        for n in range(2):
            first(c, n)
            if c == 0 and n == 0:
                pl.semaphore_wait(barrier, 24)
            send_y(c, n)
    loads[1].wait()
    loads[2].wait()

    def gather_x(c, n):
        two = pl.ds(n * 2, 2)
        own = pl.ds(pl.multiple_of(xc * 8, 8), 8)
        wait(r1.at[c, two, pl.ds(0, 7)], y_sem.at[c * 2 + n])
        for d in ORDER:
            t, who = at_x(d)
            remote(
                r1.at[c, two, :, pl.ds(pl.multiple_of(t * 8, 8), 8), :],
                a.at[c, two, :, own, :],
                send.at[1], x_sem.at[c * 2 + n], who,
            )
        a[c, two, :, own, :] = r1[c, two, :, own, :]
        wait(a.at[c, two, pl.ds(0, 7)], x_sem.at[c * 2 + n])

    def second(c, n):
        def tile(t, carry):
            for half in range(2):
                for quad in range(2):
                    for pair in range(2):
                        parts = []
                        for i in range(4):
                            rows = pl.ds(quad * 4 + i, 8, stride=8)
                            s = half * 4 + pair * 2
                            parts.append(jnp.concatenate([a[c, t, s, rows, :], a[c, t, s + 1, rows, :]], axis=0))
                        lanes = slice((half * 2 + quad) * 128, (half * 2 + quad + 1) * 128)
                        for j, part in enumerate(swap_groups(parts)):
                            high = part.astype(jnp.bfloat16)
                            low = (part - high.astype(jnp.float32)).astype(jnp.bfloat16)
                            rows = pl.ds(pl.multiple_of(t * 128 + (j * 32 + pair * 16), 16), 16)
                            bh[rows, lanes] = high
                            bl[rows, lanes] = low
            return carry

        lax.fori_loop(2 * n, 2 * n + 2, tile, 0)
        depth = slice(n * 256, (n + 1) * 256)
        for o in range(2):
            rows = pl.ds(pl.multiple_of((u if o else 1 - u) * 256, 256), 256)
            got = jnp.dot(tab[2, rows, depth], bh[depth, :], preferred_element_type=jnp.float32)
            got += jnp.dot(tab[3, rows, depth], bh[depth, :], preferred_element_type=jnp.float32)
            got += jnp.dot(tab[2, rows, depth], bl[depth, :], preferred_element_type=jnp.float32)
            got = got.reshape(8, 32, 512)
            if n == 0:
                out2[c, o] = got
            else:
                out2[c, o] += got
                for d in ORDER:
                    t, who = at_z(d)
                    remote(out2.at[c, o, t], cc.at[c, o, z], send.at[2], z_sem.at[c * 2 + o], who)
                cc[c, o, z] = out2[c, o, z]

    def third(c, o):
        wait(cc.at[c, o, pl.ds(0, 7)], z_sem.at[c * 2 + o])
        for quad in range(2):
            for half in range(2):
                for zq in range(2):
                    lanes = slice((half * 2 + quad) * 128, (half * 2 + quad + 1) * 128)
                    into = slice((half * 2 + zq) * 128, (half * 2 + zq + 1) * 128)
                    parts = [cc[c, o, zq * 4 + k, :, lanes] for k in range(4)]
                    for i, part in enumerate(swap_groups(parts)):
                        high = part.astype(jnp.bfloat16)
                        rows = slice((quad * 4 + i) * 32, (quad * 4 + i + 1) * 32)
                        ch[rows, into] = high
                        cl[rows, into] = (part - high.astype(jnp.float32)).astype(jnp.bfloat16)
        got = jnp.dot(ch[...], tab[4], preferred_element_type=jnp.float32)
        got += jnp.dot(cl[...], tab[4], preferred_element_type=jnp.float32)
        got += jnp.dot(ch[...], tab[5], preferred_element_type=jnp.float32)
        return (0.5 * got * got).reshape(8, 32, 512)

    def step(c, carry):
        for n in range(2):
            gather_x(c, n)
            second(c, n)

        @pl.when(c > 0)
        def _():
            def half(o, carry):
                level = third(c - 1, o)
                acc[o] = jnp.where(c == 1, level, acc[o] + level)
                return carry

            lax.fori_loop(0, 2, half, 0)

        return carry

    lax.fori_loop(0, 3, step, 0)

    slot = pl.ds(1 + u * 8, 8)
    other = pl.ds(1 + (1 - u) * 8, 8)

    acc[0] += third(2, 0)
    remote(acc.at[0], ext.at[slot], send.at[3], e_sem.at[0], partner)
    top, bottom = acc[0, :, 0, :], acc[0, :, 31, :]
    edge[2] = jnp.where(u == 0, bottom, top)
    remote(edge.at[2], halo.at[u, u], send.at[4], h_sem.at[4], beyond)
    halo[1 - u, u] = jnp.where(u == 0, top, bottom)

    acc[1] += third(2, 1)
    top, bottom = acc[1, :, 0, :], acc[1, :, 31, :]
    edge[0] = jnp.where(u == 0, bottom, top)
    edge[1] = jnp.where(u == 0, top, bottom)
    remote(edge.at[0], halo.at[u, u], send.at[5], h_sem.at[2], partner)
    remote(edge.at[1], halo.at[1 - u, u], send.at[6], h_sem.at[3], beside)
    ext[slot] = acc[1]

    place = lax.broadcasted_iota(jnp.int32, (32, 512), 0)

    def plane(i, carry):
        centre = ext[i + 1]
        step_x = 0.5 * (ext[i + 2] - ext[i])
        after = jnp.where(place == 31, halo[1, i // 8, pl.ds(i % 8, 1), :], pltpu.roll(centre, 31, 0))
        before = jnp.where(place == 0, halo[0, i // 8, pl.ds(i % 8, 1), :], pltpu.roll(centre, 1, 0))
        step_y = 0.5 * (after - before)
        step_z = 0.5 * (pltpu.roll(centre, 511, 1) - pltpu.roll(centre, 1, 1))
        square = step_x * step_x + step_y * step_y + step_z * step_z
        scale = -lax.rsqrt(jnp.maximum(square, 1.0))
        nrm[0, i] = (step_x * scale).astype(jnp.bfloat16)
        nrm[1, i] = (step_y * scale).astype(jnp.bfloat16)
        nrm[2, i] = (step_z * scale).astype(jnp.bfloat16)
        return carry

    wait(halo.at[0, 0], h_sem.at[4])
    lax.fori_loop(1 + 8 * u, 7 + 8 * u, plane, 0)

    wait(halo.at[0, 0], h_sem.at[2])
    wait(halo.at[0, 0], h_sem.at[3])
    wait(ext.at[pl.ds(1, 8)], e_sem.at[0])
    remote(ext.at[16], ext.at[0], send.at[7], h_sem.at[0], up)
    remote(ext.at[1], ext.at[17], send.at[8], h_sem.at[1], down)
    level_out = pltpu.make_async_copy(ext.at[pl.ds(1, 16)], e_ref, store.at[0])
    level_out.start()
    lax.fori_loop(7 - 6 * u, 15 - 6 * u, plane, 0)
    inner = pl.ds(1, 14)
    inner_out = pltpu.make_async_copy(nrm.at[:, inner], n_ref.at[:, inner], store.at[1])
    inner_out.start()
    wait(ext.at[0], h_sem.at[0])
    wait(ext.at[17], h_sem.at[1])
    outs = []
    for k, i in enumerate((0, 15)):
        plane(i, 0)
        outs.append(pltpu.make_async_copy(nrm.at[:, i], n_ref.at[:, i], store.at[2 + k]))
        outs[-1].start()

    wait(out1.at[:, :, pl.ds(0, 7)], send.at[0])
    wait(a.at[:, :, pl.ds(0, 7)], send.at[1])
    wait(out2.at[:, :, pl.ds(0, 7)], send.at[2])
    wait(acc.at[0], send.at[3])
    wait(edge.at[0], send.at[4])
    wait(edge.at[0], send.at[5])
    wait(edge.at[0], send.at[6])
    wait(ext.at[16], send.at[7])
    wait(ext.at[1], send.at[8])
    level_out.wait()
    inner_out.wait()
    for out in outs:
        out.wait()


def body(coefficients):
    members, span_b, span_q, length = coefficients.shape
    data = coefficients.reshape(members, span_b * span_q, length)
    apart = pl.BlockSpec(memory_space=pl.ANY)
    f32, bf16 = jnp.float32, jnp.bfloat16
    return pl.pallas_call(
        kernel,
        out_shape=(
            jax.ShapeDtypeStruct((16, 32, 512), f32),
            jax.ShapeDtypeStruct((3, 16, 32, 512), bf16),
        ),
        in_specs=[pl.BlockSpec(memory_space=pltpu.HBM)] * 2,
        out_specs=(apart, apart),
        scratch_shapes=[
            pltpu.VMEM((3, 512, 512), bf16),
            pltpu.VMEM((6, 512, 512), bf16),
            pltpu.VMEM((3, 4, 8, 64, 128), f32),
            pltpu.VMEM((3, 4, 8, 64, 128), f32),
            pltpu.VMEM((3, 4, 8, 64, 128), f32),
            pltpu.VMEM((512, 512), bf16),
            pltpu.VMEM((512, 512), bf16),
            pltpu.VMEM((3, 2, 8, 32, 512), f32),
            pltpu.VMEM((3, 2, 8, 32, 512), f32),
            pltpu.VMEM((256, 512), bf16),
            pltpu.VMEM((256, 512), bf16),
            pltpu.VMEM((2, 8, 32, 512), f32),
            pltpu.VMEM((18, 32, 512), f32),
            pltpu.VMEM((3, 8, 512), f32),
            pltpu.VMEM((2, 2, 8, 512), f32),
            pltpu.VMEM((3, 16, 32, 512), bf16),
            pltpu.SemaphoreType.DMA((6,)),
            pltpu.SemaphoreType.DMA((4,)),
            pltpu.SemaphoreType.DMA((9,)),
            pltpu.SemaphoreType.DMA((6,)),
            pltpu.SemaphoreType.DMA((6,)),
            pltpu.SemaphoreType.DMA((6,)),
            pltpu.SemaphoreType.DMA((1,)),
            pltpu.SemaphoreType.DMA((5,)),
        ],
        compiler_params=pltpu.CompilerParams(
            collective_id=0, has_side_effects=True, vmem_limit_bytes=VMEM_MIB * 1024 * 1024
        ),
        name="vorticity_normals",
    )(data, tables(length))


def solution(mesh):
    return jax.shard_map(
        body,
        mesh=mesh,
        in_specs=(P(None, "row", "col", None),),
        out_specs=(P("row", "col", None), P(None, "row", "col", None)),
        check_vma=False,
    )
```

time: 170 us -> 148 us (0.87)
  Pallas kernels: 165 us -> 141 us
  local copies, waits for them, and re-layouts: 3.55 us -> 5.41 us
    pallas_call x1, Pallas kernels: 165 us -> 141 us  [body(): pl.pallas_call(kernel, out_shape=(jax.ShapeDtypeStruct((16, 32, 512), f32...]
    unnamed x4 -> x6, local copies, waits for them, and re-layouts: 3.55 us -> 5.41 us
where the time goes in v1:
time: 148 us; the launch traced here: 147 us
  Pallas kernels  141 us (95%)
  local copies, waits for them, and re-layouts  5.41 us (4%)
    pallas_call x1, Pallas kernels, body(): pl.pallas_call(kernel, out_shape=(jax.ShapeDtypeStruct((16, 32, 512), f32...  141 us
    unnamed x6, local copies, waits for them, and re-layouts  5.41 us

profile of v1, /device:TPU:1, one launch (start us, length us, event | category | flops | bytes accessed | tf_op | source)
XLA Modules:
  0.0 147.2 jit_solution(17851216221305739691)
XLA Ops:
  0.6 0.0 copy-start
  0.6 1.9 %copy-done = bf16[6,512,512]{2,1,0:T(8,128)(2,1)S(1)} copy-done((bf16[6,512,512]{2,1,0:T(8,128)(2,1)S(1)}, bf16[6,512,512]{2,1,0:T(8,128)(2,1)}, u32[]{:S(2)}) %copy-start) | copy-done | bytes 3145752
  2.5 0.0 copy-start.1
  2.5 1.4 copy-done.1
  3.9 141.1 %vorticity_normals.1 = (f32[16,32,512]{2,1,0:T(8,128)S(1)}, bf16[3,16,32,512]{3,2,1,0:T(8,128)(2,1)S(1)}) custom-call(bf16[3,512,512]{2,1,0:T(8,128)(2,1)S(1)} %bitcast.1, bf16[6,512,512]{2,1,0:T(8,128)(2,1)S(1)} %copy-done), custom_call_target="tpu_custom_call" | custom-call | tf_op jit(solution)/shard_map/vorticity_normals/pallas_call | solution.py:303
  145.1 1.0 copy.6
  146.0 1.1 copy.7
Async XLA Ops:
  0.6 1.9 %copy-start = (bf16[6,512,512]{2,1,0:T(8,128)(2,1)S(1)}, bf16[6,512,512]{2,1,0:T(8,128)(2,1)}, u32[]{:S(2)}) copy-start(bf16[6,512,512]{2,1,0:T(8,128)(2,1)} %constant.2.clone.t_hbm) | copy-start | bytes 9437188
  2.5 1.4 copy-start.1

commit v2 on v1

v2 whole, which is shorter than its diff:
```python
import functools

import jax
import jax.numpy as jnp
import numpy as np
from jax import lax
from jax.experimental import pallas as pl
from jax.experimental.pallas import tpu as pltpu
from jax.sharding import PartitionSpec as P

MESH = pl.DeviceIdType.MESH
NT = (((1,), (1,)), ((), ()))
VMEM_MIB = 51
CHUNKS = ((0, 1, 6, 7), (2, 3, 4, 5))
ORDER = (4, 3, 5, 2, 6, 1, 7)


def fourier_table(n):
    k = np.arange(n)[:, None]
    x = np.arange(n)[None, :]
    h = n // 2
    f = np.where(k <= h, k, k - h)
    angle = (f * x % n) * (2.0 * np.pi / n)
    weight = np.where((k == 0) | (k == h), np.sqrt(1.0 / n), np.sqrt(2.0 / n))
    return (np.where(k <= h, np.cos(angle), np.sin(angle)) * weight).astype(np.float32)


def split(table):
    high = table.astype(jnp.bfloat16)
    low = (table - high.astype(np.float32)).astype(jnp.bfloat16)
    return high, low


def tables(n):
    t = fourier_table(n)
    planes = np.array(CHUNKS)
    k, p, xc, i = np.meshgrid(np.arange(2), np.arange(8), np.arange(8), np.arange(4), indexing="ij")
    x_order = (((p % 4) * 8 + xc) * 16 + (p // 4) * 8 + planes[k, i]).reshape(-1)
    h, zs, j = np.meshgrid(np.arange(2), np.arange(8), np.arange(32), indexing="ij")
    y_order = (zs * 64 + h * 32 + j).reshape(-1)
    bi, g = np.meshgrid(np.arange(16), np.arange(32), indexing="ij")
    b_order = (g * 16 + bi).reshape(-1)
    yh, zs, qj = np.meshgrid(np.arange(2), np.arange(8), np.arange(32), indexing="ij")
    q_order = ((zs * 2 + yh) * 32 + qj).reshape(-1)
    first = split(np.ascontiguousarray(t[:, x_order].T))
    second = split(np.ascontiguousarray(t[b_order][:, y_order].T))
    third = split(np.ascontiguousarray(t[q_order]))
    return np.stack(first + second + third)


def swap_groups(parts):
    lane = lax.broadcasted_iota(jnp.int32, parts[0].shape, 1)
    low_half = lane < 64
    even = (lane // 32) % 2 == 0
    p0, p1, p2, p3 = parts
    a0 = jnp.where(low_half, p0, pltpu.roll(p2, 64, 1))
    a2 = jnp.where(low_half, pltpu.roll(p0, 64, 1), p2)
    a1 = jnp.where(low_half, p1, pltpu.roll(p3, 64, 1))
    a3 = jnp.where(low_half, pltpu.roll(p1, 64, 1), p3)
    out = []
    for u, v in ((a0, a1), (a2, a3)):
        out.append(jnp.where(even, u, pltpu.roll(v, 32, 1)))
        out.append(jnp.where(even, pltpu.roll(u, 96, 1), v))
    return out


def kernel(
    x_hbm, t_hbm, e_ref, n_ref,
    x_ref, tab, out1, r1, a, bh, bl, out2, cc, ch, cl, acc, ext, edge, halo, nrm,
    load, store, send, y_sem, x_sem, z_sem, e_sem, h_sem,
):
    row = lax.axis_index("row")
    col = lax.axis_index("col")
    y_lo, xc = row // 8, row % 8
    z, u = col // 2, col % 2
    y = u * 4 + y_lo

    def at_y(d):
        t = (y + d) % 8
        return t, {"row": (t % 4) * 8 + xc, "col": z * 2 + t // 4}

    def at_x(d):
        t = (xc + d) % 8
        return t, {"row": y_lo * 8 + t, "col": col}

    def at_z(d):
        t = (z + d) % 8
        return t, {"row": row, "col": t * 2 + u}

    partner = at_y(4)[1]
    up = {"row": (row + 1) % 32, "col": col}
    down = {"row": (row + 31) % 32, "col": col}
    beside = {"row": row, "col": (col + 15 + 2 * u) % 16}
    beyond = {"row": row, "col": (col + 2 + 12 * u) % 16}

    barrier = pltpu.get_barrier_semaphore()
    for d in ORDER:
        for at in (at_y, at_x, at_z):
            pl.semaphore_signal(barrier, inc=1, device_id=at(d)[1], device_id_type=MESH)
    for who in (up, down, beside):
        pl.semaphore_signal(barrier, inc=1, device_id=who, device_id_type=MESH)

    def wait(ref, sem):
        pltpu.make_async_copy(ref, ref, sem).wait()

    loads = [pltpu.make_async_copy(t_hbm.at[pl.ds(2 * i, 2)], tab.at[pl.ds(2 * i, 2)], load.at[i]) for i in range(3)]
    loads += [pltpu.make_async_copy(x_hbm.at[c], x_ref.at[c], load.at[3 + c]) for c in range(3)]
    for i in (0, 3, 4, 5, 1, 2):
        loads[i].start()

    def remote(src, dst, s, r, who):
        pltpu.make_async_remote_copy(
            src_ref=src, dst_ref=dst, send_sem=s, recv_sem=r, device_id=who, device_id_type=MESH
        ).start()

    upper = lax.broadcasted_iota(jnp.int32, (32, 8, 256), 1) < 4

    def first(c, k):
        rows = slice(k * 256, (k + 1) * 256)
        got = []
        for w in range(2):
            data = x_ref[c, w * 256 : (w + 1) * 256, :]
            part = lax.dot_general(tab[0, rows, :], data, NT, preferred_element_type=jnp.float32)
            part += lax.dot_general(tab[1, rows, :], data, NT, preferred_element_type=jnp.float32)
            got.append(part.reshape(32, 8, 256))
        even = jnp.where(upper, got[0], pltpu.roll(got[1], 4, 1))
        odd = jnp.where(upper, pltpu.roll(got[0], 4, 1), got[1])
        both = jnp.stack([even, odd], axis=1)
        for t in range(2):
            out1[c, k, t] = both[:, :, :, t * 128 : (t + 1) * 128].reshape(8, 64, 128)

    def send_y(c, k):
        for d in ORDER:
            t, who = at_y(d)
            remote(out1.at[c, k, :, t], r1.at[c, k, :, y], send.at[0], y_sem.at[k * 3 + c], who)
        r1[c, k, :, y] = out1[c, k, :, y]

    loads[0].wait()
    for k in range(2):
        for c in range(3):
            if k == 0:
                loads[3 + c].wait()
            first(c, k)
            if c == 0 and k == 0:
                pl.semaphore_wait(barrier, 24)
            send_y(c, k)
    loads[1].wait()
    loads[2].wait()

    def gather_x(c, k):
        own = pl.ds(pl.multiple_of(xc * 8, 8), 8)
        wait(r1.at[c, k, :, pl.ds(0, 7)], y_sem.at[k * 3 + c])
        for d in ORDER:
            t, who = at_x(d)
            remote(
                r1.at[c, k, :, :, pl.ds(pl.multiple_of(t * 8, 8), 8), :],
                a.at[c, k, :, :, own, :],
                send.at[1], x_sem.at[k * 3 + c], who,
            )
        a[c, k, :, :, own, :] = r1[c, k, :, :, own, :]
        wait(a.at[c, k, :, pl.ds(0, 7)], x_sem.at[k * 3 + c])

    def second(c, k):
        def tile(t, carry):
            for w in range(2):
                for half in range(2):
                    for pair in range(2):
                        parts = []
                        for i in range(4):
                            rows = pl.ds(w * 4 + i, 8, stride=8)
                            s = half * 4 + pair * 2
                            parts.append(
                                jnp.concatenate([a[c, k, t, s, rows, :], a[c, k, t, s + 1, rows, :]], axis=0)
                            )
                        lanes = slice(half * 128, (half + 1) * 128)
                        for j, part in enumerate(swap_groups(parts)):
                            high = part.astype(jnp.bfloat16)
                            low = (part - high.astype(jnp.float32)).astype(jnp.bfloat16)
                            rows = pl.ds(pl.multiple_of(t * 128 + (w * 256 + j * 32 + pair * 16), 16), 16)
                            bh[rows, lanes] = high
                            bl[rows, lanes] = low
            return carry

        lax.fori_loop(0, 2, tile, 0)
        for o in range(2):
            rows = pl.ds(pl.multiple_of((u if o else 1 - u) * 256, 256), 256)
            got = jnp.dot(tab[2, rows, :], bh[...], preferred_element_type=jnp.float32)
            got += jnp.dot(tab[3, rows, :], bh[...], preferred_element_type=jnp.float32)
            got += jnp.dot(tab[2, rows, :], bl[...], preferred_element_type=jnp.float32)
            out2[c, k, o] = got.reshape(8, 32, 256)
            for d in ORDER:
                t, who = at_z(d)
                remote(
                    out2.at[c, k, o, t], cc.at[c, k, o, z],
                    send.at[2], z_sem.at[(k * 3 + c) * 2 + o], who,
                )
            cc[c, k, o, z] = out2[c, k, o, z]

    def third(c, k, o):
        wait(cc.at[c, k, o, pl.ds(0, 7)], z_sem.at[(k * 3 + c) * 2 + o])
        for half in range(2):
            for zq in range(2):
                lanes = slice(half * 128, (half + 1) * 128)
                into = slice((half * 2 + zq) * 128, (half * 2 + zq + 1) * 128)
                parts = [cc[c, k, o, zq * 4 + i, :, lanes] for i in range(4)]
                for i, part in enumerate(swap_groups(parts)):
                    high = part.astype(jnp.bfloat16)
                    rows = slice(i * 32, (i + 1) * 32)
                    ch[rows, into] = high
                    cl[rows, into] = (part - high.astype(jnp.float32)).astype(jnp.bfloat16)
        got = jnp.dot(ch[...], tab[4], preferred_element_type=jnp.float32)
        got += jnp.dot(cl[...], tab[4], preferred_element_type=jnp.float32)
        got += jnp.dot(ch[...], tab[5], preferred_element_type=jnp.float32)
        level = (0.5 * got * got).reshape(4, 32, 512)
        acc[k, o] = jnp.where(c == 0, level, acc[k, o] + level)

    base = 1 + u * 8

    def step(j, carry):
        @pl.when(j < 6)
        def _():
            gather_x(j % 3, j // 3)
            second(j % 3, j // 3)

        @pl.when(j > 1)
        def _():
            c, k = (j - 2) % 3, (j - 2) // 3

            def half(o, carry):
                third(c, k, o)

                @pl.when((c == 2) & (k == 0) & (o == 0))
                def _():
                    for i in (0, 2):
                        planes = pl.ds(base + 3 * i, 2)
                        remote(acc.at[0, 0, pl.ds(i, 2)], ext.at[planes], send.at[3], e_sem.at[0], partner)

                @pl.when((c == 2) & (k == 1) & (o == 0))
                def _():
                    remote(acc.at[1, 0], ext.at[pl.ds(base + 2, 4)], send.at[3], e_sem.at[1], partner)

                return carry

            lax.fori_loop(0, 2, half, 0)

        return carry

    lax.fori_loop(0, 8, step, 0)

    def line(o, r):
        first_four, last_four = acc[0, o, :, r, :], acc[1, o, :, r, :]
        return jnp.concatenate([first_four[:2], last_four, first_four[2:]], axis=0)

    top, bottom = line(0, 0), line(0, 31)
    edge[2] = jnp.where(u == 0, bottom, top)
    remote(edge.at[2], halo.at[u, u], send.at[4], h_sem.at[4], beyond)
    halo[1 - u, u] = jnp.where(u == 0, top, bottom)
    top, bottom = line(1, 0), line(1, 31)
    edge[0] = jnp.where(u == 0, bottom, top)
    edge[1] = jnp.where(u == 0, top, bottom)
    remote(edge.at[0], halo.at[u, u], send.at[5], h_sem.at[2], partner)
    remote(edge.at[1], halo.at[1 - u, u], send.at[6], h_sem.at[3], beside)
    for k in range(2):
        for i, at in enumerate(CHUNKS[k]):
            ext[base + at] = acc[k, 1, i]

    place = lax.broadcasted_iota(jnp.int32, (32, 512), 0)

    def plane(i, carry):
        centre = ext[i + 1]
        step_x = 0.5 * (ext[i + 2] - ext[i])
        after = jnp.where(place == 31, halo[1, i // 8, pl.ds(i % 8, 1), :], pltpu.roll(centre, 31, 0))
        before = jnp.where(place == 0, halo[0, i // 8, pl.ds(i % 8, 1), :], pltpu.roll(centre, 1, 0))
        step_y = 0.5 * (after - before)
        step_z = 0.5 * (pltpu.roll(centre, 511, 1) - pltpu.roll(centre, 1, 1))
        square = step_x * step_x + step_y * step_y + step_z * step_z
        scale = -lax.rsqrt(jnp.maximum(square, 1.0))
        nrm[0, i] = (step_x * scale).astype(jnp.bfloat16)
        nrm[1, i] = (step_y * scale).astype(jnp.bfloat16)
        nrm[2, i] = (step_z * scale).astype(jnp.bfloat16)
        return carry

    wait(ext.at[pl.ds(1, 4)], e_sem.at[0])
    remote(ext.at[16], ext.at[0], send.at[7], h_sem.at[0], up)
    remote(ext.at[1], ext.at[17], send.at[8], h_sem.at[1], down)
    mine, theirs = pl.ds(8 * u, 8), pl.ds(8 * (1 - u), 8)
    level_mine = pltpu.make_async_copy(ext.at[pl.ds(base, 8)], e_ref.at[mine], store.at[0])
    level_mine.start()
    wait(halo.at[0, 0], h_sem.at[4])
    lax.fori_loop(1 + 8 * u, 7 + 8 * u, plane, 0)
    wait(halo.at[0, 0], h_sem.at[2])
    wait(halo.at[0, 0], h_sem.at[3])
    lax.fori_loop(7, 9, plane, 0)
    wait(ext.at[0], h_sem.at[0])
    wait(ext.at[17], h_sem.at[1])
    plane(0, 0)
    plane(15, 0)
    normals_mine = pltpu.make_async_copy(nrm.at[:, mine], n_ref.at[:, mine], store.at[1])
    normals_mine.start()
    wait(ext.at[pl.ds(1, 4)], e_sem.at[1])
    level_theirs = pltpu.make_async_copy(ext.at[pl.ds(9 - 8 * u, 8)], e_ref.at[theirs], store.at[2])
    level_theirs.start()
    lax.fori_loop(9 - 8 * u, 15 - 8 * u, plane, 0)
    normals_theirs = pltpu.make_async_copy(nrm.at[:, theirs], n_ref.at[:, theirs], store.at[3])
    normals_theirs.start()

    wait(out1.at[:, :, :, pl.ds(0, 7)], send.at[0])
    wait(a.at[:, :, :, pl.ds(0, 7)], send.at[1])
    wait(out2.at[:, :, :, pl.ds(0, 7)], send.at[2])
    wait(acc.at[0], send.at[3])
    wait(edge.at[0], send.at[4])
    wait(edge.at[0], send.at[5])
    wait(edge.at[0], send.at[6])
    wait(ext.at[16], send.at[7])
    wait(ext.at[1], send.at[8])
    for out in (level_mine, normals_mine, level_theirs, normals_theirs):
        out.wait()


def body(coefficients):
    members, span_b, span_q, length = coefficients.shape
    data = coefficients.reshape(members, span_b * span_q, length)
    apart = pl.BlockSpec(memory_space=pl.ANY)
    f32, bf16 = jnp.float32, jnp.bfloat16
    return pl.pallas_call(
        kernel,
        out_shape=(
            jax.ShapeDtypeStruct((16, 32, 512), f32),
            jax.ShapeDtypeStruct((3, 16, 32, 512), bf16),
        ),
        in_specs=[pl.BlockSpec(memory_space=pltpu.HBM)] * 2,
        out_specs=(apart, apart),
        scratch_shapes=[
            pltpu.VMEM((3, 512, 512), bf16),
            pltpu.VMEM((6, 512, 512), bf16),
            pltpu.VMEM((3, 2, 2, 8, 64, 128), f32),
            pltpu.VMEM((3, 2, 2, 8, 64, 128), f32),
            pltpu.VMEM((3, 2, 2, 8, 64, 128), f32),
            pltpu.VMEM((512, 256), bf16),
            pltpu.VMEM((512, 256), bf16),
            pltpu.VMEM((3, 2, 2, 8, 32, 256), f32),
            pltpu.VMEM((3, 2, 2, 8, 32, 256), f32),
            pltpu.VMEM((128, 512), bf16),
            pltpu.VMEM((128, 512), bf16),
            pltpu.VMEM((2, 2, 4, 32, 512), f32),
            pltpu.VMEM((18, 32, 512), f32),
            pltpu.VMEM((3, 8, 512), f32),
            pltpu.VMEM((2, 2, 8, 512), f32),
            pltpu.VMEM((3, 16, 32, 512), bf16),
            pltpu.SemaphoreType.DMA((6,)),
            pltpu.SemaphoreType.DMA((4,)),
            pltpu.SemaphoreType.DMA((9,)),
            pltpu.SemaphoreType.DMA((6,)),
            pltpu.SemaphoreType.DMA((6,)),
            pltpu.SemaphoreType.DMA((12,)),
            pltpu.SemaphoreType.DMA((2,)),
            pltpu.SemaphoreType.DMA((5,)),
        ],
        compiler_params=pltpu.CompilerParams(
            collective_id=0, has_side_effects=True, vmem_limit_bytes=VMEM_MIB * 1024 * 1024
        ),
        name="vorticity_normals",
    )(data, tables(length))


def solution(mesh):
    return jax.shard_map(
        body,
        mesh=mesh,
        in_specs=(P(None, "row", "col", None),),
        out_specs=(P("row", "col", None), P(None, "row", "col", None)),
        check_vma=False,
    )
```

time: 148 us -> 127 us (0.86)
  Pallas kernels: 141 us -> 124 us
  local copies, waits for them, and re-layouts: 5.41 us -> 2.11 us
    pallas_call x1, Pallas kernels: 141 us -> 124 us  [body(): pl.pallas_call(kernel, out_shape=(jax.ShapeDtypeStruct((16, 32, 512), f32...]
    unnamed x6 -> x2, local copies, waits for them, and re-layouts: 5.41 us -> 2.11 us
where the time goes in v2:
time: 127 us
  Pallas kernels  124 us (98%)
  local copies, waits for them, and re-layouts  2.11 us (2%)
    pallas_call x1, Pallas kernels, body(): pl.pallas_call(kernel, out_shape=(jax.ShapeDtypeStruct((16, 32, 512), f32...  124 us

profile of v2, /device:TPU:1, one launch (start us, length us, event | category | flops | bytes accessed | tf_op | source)
XLA Modules:
  0.0 126.7 jit_solution(5326069772523586596)
XLA Ops:
  0.6 124.0 %vorticity_normals.1 = (f32[16,32,512]{2,1,0:T(8,128)S(1)}, bf16[3,16,32,512]{3,2,1,0:T(8,128)(2,1)S(1)}) custom-call(bf16[3,512,512]{2,1,0:T(8,128)(2,1)} %bitcast.1, bf16[6,512,512]{2,1,0:T(8,128)(2,1)} %constant.2.clone.t_hbm), custom_call_target="tpu_custom_call" | custom-call | tf_op jit(solution)/shard_map/vorticity_normals/pallas_call | solution.py:325
  124.6 1.0 copy.6
  125.6 1.1 copy.7

commit v3 on v2

v3 whole, which is shorter than its diff:
```python
import functools

import jax
import jax.numpy as jnp
import numpy as np
from jax import lax
from jax.experimental import pallas as pl
from jax.experimental.pallas import tpu as pltpu
from jax.sharding import PartitionSpec as P

MESH = pl.DeviceIdType.MESH
NT = (((1,), (1,)), ((), ()))
VMEM_MIB = 51
CHUNKS = ((0, 7), (1, 6), (2, 5), (3, 4))
ORDER = (4, 3, 5, 2, 6, 1, 7)


def fourier_table(n):
    k = np.arange(n)[:, None]
    x = np.arange(n)[None, :]
    h = n // 2
    f = np.where(k <= h, k, k - h)
    angle = (f * x % n) * (2.0 * np.pi / n)
    weight = np.where((k == 0) | (k == h), np.sqrt(1.0 / n), np.sqrt(2.0 / n))
    return (np.where(k <= h, np.cos(angle), np.sin(angle)) * weight).astype(np.float32)


def split(table):
    high = table.astype(jnp.bfloat16)
    low = (table - high.astype(np.float32)).astype(jnp.bfloat16)
    return high, low


def tables(n):
    t = fourier_table(n)
    planes = np.array(CHUNKS)
    k, p, xc, i = np.meshgrid(np.arange(4), np.arange(8), np.arange(8), np.arange(2), indexing="ij")
    x_order = (((p % 4) * 8 + xc) * 16 + (p // 4) * 8 + planes[k, i]).reshape(-1)
    h, zs, j = np.meshgrid(np.arange(2), np.arange(8), np.arange(32), indexing="ij")
    y_order = (zs * 64 + h * 32 + j).reshape(-1)
    bi, g = np.meshgrid(np.arange(16), np.arange(32), indexing="ij")
    b_order = (g * 16 + bi).reshape(-1)
    yh, zs, qj = np.meshgrid(np.arange(2), np.arange(8), np.arange(32), indexing="ij")
    q_order = ((zs * 2 + yh) * 32 + qj).reshape(-1)
    first = split(np.ascontiguousarray(t[:, x_order].T))
    second = split(np.ascontiguousarray(t[b_order][:, y_order].T))
    third = split(np.ascontiguousarray(t[q_order]))
    return np.stack(first + second + third)


def swap_groups(parts, axis, size):
    unit = size // 4
    at = lax.broadcasted_iota(jnp.int32, parts[0].shape, axis)
    low_half = at < 2 * unit
    even = (at // unit) % 2 == 0
    p0, p1, p2, p3 = parts
    a0 = jnp.where(low_half, p0, pltpu.roll(p2, 2 * unit, axis))
    a2 = jnp.where(low_half, pltpu.roll(p0, 2 * unit, axis), p2)
    a1 = jnp.where(low_half, p1, pltpu.roll(p3, 2 * unit, axis))
    a3 = jnp.where(low_half, pltpu.roll(p1, 2 * unit, axis), p3)
    out = []
    for u, v in ((a0, a1), (a2, a3)):
        out.append(jnp.where(even, u, pltpu.roll(v, unit, axis)))
        out.append(jnp.where(even, pltpu.roll(u, 3 * unit, axis), v))
    return out


def kernel(
    x_hbm, t_hbm, e_ref, n_ref,
    x_ref, tab, out1, r1, a, bh, bl, out2, cc, ch, cl, acc, ext, edge, halo, nrm,
    load, store, send, y_sem, x_sem, z_sem, e_sem, h_sem,
):
    row = lax.axis_index("row")
    col = lax.axis_index("col")
    y_lo, xc = row // 8, row % 8
    z, u = col // 2, col % 2
    y = u * 4 + y_lo

    def at_y(d):
        t = (y + d) % 8
        return t, {"row": (t % 4) * 8 + xc, "col": z * 2 + t // 4}

    def at_x(d):
        t = (xc + d) % 8
        return t, {"row": y_lo * 8 + t, "col": col}

    def at_z(d):
        t = (z + d) % 8
        return t, {"row": row, "col": t * 2 + u}

    partner = at_y(4)[1]
    up = {"row": (row + 1) % 32, "col": col}
    down = {"row": (row + 31) % 32, "col": col}
    beside = {"row": row, "col": (col + 15 + 2 * u) % 16}
    beyond = {"row": row, "col": (col + 2 + 12 * u) % 16}

    barrier = pltpu.get_barrier_semaphore()
    for d in ORDER:
        for at in (at_y, at_x, at_z):
            pl.semaphore_signal(barrier, inc=1, device_id=at(d)[1], device_id_type=MESH)
    for who in (up, down, beside):
        pl.semaphore_signal(barrier, inc=1, device_id=who, device_id_type=MESH)

    def wait(ref, sem):
        pltpu.make_async_copy(ref, ref, sem).wait()

    loads = [pltpu.make_async_copy(t_hbm.at[pl.ds(2 * i, 2)], tab.at[pl.ds(2 * i, 2)], load.at[i]) for i in range(3)]
    loads += [pltpu.make_async_copy(x_hbm.at[c], x_ref.at[c], load.at[3 + c]) for c in range(3)]
    for i in (0, 3, 4, 5, 1, 2):
        loads[i].start()

    def remote(src, dst, s, r, who):
        pltpu.make_async_remote_copy(
            src_ref=src, dst_ref=dst, send_sem=s, recv_sem=r, device_id=who, device_id_type=MESH
        ).start()

    def first(c, k):
        rows = slice(k * 128, (k + 1) * 128)
        got = lax.dot_general(tab[0, rows, :], x_ref[c], NT, preferred_element_type=jnp.float32)
        got += lax.dot_general(tab[1, rows, :], x_ref[c], NT, preferred_element_type=jnp.float32)
        parts = [got[:, w * 128 : (w + 1) * 128].reshape(16, 8, 128) for w in range(4)]
        out1[c, k] = jnp.stack(swap_groups(parts, 1, 8), axis=1).reshape(8, 64, 128)

    def send_y(c, k):
        for d in ORDER:
            t, who = at_y(d)
            remote(out1.at[c, k, t], r1.at[c, k, y], send.at[0], y_sem.at[k * 3 + c], who)
        r1[c, k, y] = out1[c, k, y]

    loads[0].wait()
    for k in range(4):
        for c in range(3):
            if k == 0:
                loads[3 + c].wait()
            first(c, k)
            if c == 0 and k == 0:
                pl.semaphore_wait(barrier, 24)
            send_y(c, k)
    loads[1].wait()
    loads[2].wait()

    def send_x(j):
        c, k = j % 3, j // 3
        own = pl.ds(pl.multiple_of(xc * 8, 8), 8)
        wait(r1.at[c, k, pl.ds(0, 7)], y_sem.at[j])
        for d in ORDER:
            t, who = at_x(d)
            remote(
                r1.at[c, k, :, pl.ds(pl.multiple_of(t * 8, 8), 8), :],
                a.at[c, k, :, own, :],
                send.at[1], x_sem.at[j], who,
            )
        a[c, k, :, own, :] = r1[c, k, :, own, :]

    def second(j):
        c, k = j % 3, j // 3
        wait(a.at[c, k, pl.ds(0, 7)], x_sem.at[j])
        for w in range(4):
            for pair in range(2):
                parts = []
                for half in range(2):
                    for i in range(2):
                        rows = pl.ds(w * 2 + i, 8, stride=8)
                        s = half * 4 + pair * 2
                        parts.append(jnp.concatenate([a[c, k, s, rows, :], a[c, k, s + 1, rows, :]], axis=0))
                for n, part in enumerate(swap_groups(parts, 1, 128)):
                    high = part.astype(jnp.bfloat16)
                    rows = slice((w * 4 + n) * 32 + pair * 16, (w * 4 + n) * 32 + (pair + 1) * 16)
                    bh[rows, :] = high
                    bl[rows, :] = (part - high.astype(jnp.float32)).astype(jnp.bfloat16)
        for o in range(2):
            rows = pl.ds(pl.multiple_of((u if o else 1 - u) * 256, 256), 256)
            got = jnp.dot(tab[2, rows, :], bh[...], preferred_element_type=jnp.float32)
            got += jnp.dot(tab[3, rows, :], bh[...], preferred_element_type=jnp.float32)
            got += jnp.dot(tab[2, rows, :], bl[...], preferred_element_type=jnp.float32)
            out2[c, k, o] = got.reshape(8, 32, 128)
            for d in ORDER:
                t, who = at_z(d)
                remote(out2.at[c, k, o, t], cc.at[c, k, o, z], send.at[2], z_sem.at[j * 2 + o], who)
            cc[c, k, o, z] = out2[c, k, o, z]

    base = 1 + u * 8

    def third(j):
        c, k = j % 3, j // 3

        def half(o, carry):
            wait(cc.at[c, k, o, pl.ds(0, 7)], z_sem.at[j * 2 + o])
            for zq in range(2):
                parts = [cc[c, k, o, zq * 4 + i] for i in range(4)]
                for n, part in enumerate(swap_groups(parts, 1, 128)):
                    high = part.astype(jnp.bfloat16)
                    rows = slice((n % 2) * 32, (n % 2 + 1) * 32)
                    into = slice((n // 2 * 2 + zq) * 128, (n // 2 * 2 + zq + 1) * 128)
                    ch[rows, into] = high
                    cl[rows, into] = (part - high.astype(jnp.float32)).astype(jnp.bfloat16)
            got = jnp.dot(ch[...], tab[4], preferred_element_type=jnp.float32)
            got += jnp.dot(cl[...], tab[4], preferred_element_type=jnp.float32)
            got += jnp.dot(ch[...], tab[5], preferred_element_type=jnp.float32)
            level = (0.5 * got * got).reshape(2, 32, 512)
            acc[k, o] = jnp.where(c == 0, level, acc[k, o] + level)

            @pl.when((c == 2) & (o == 0))
            def _():
                remote(acc.at[k, 0, 0], ext.at[base + k], send.at[3], e_sem.at[k], partner)
                remote(acc.at[k, 0, 1], ext.at[base + 7 - k], send.at[3], e_sem.at[k], partner)

            return carry

        lax.fori_loop(0, 2, half, 0)

    def step(j, carry):
        @pl.when(j < 12)
        def _():
            send_x(j)

        @pl.when((j > 0) & (j < 13))
        def _():
            second(j - 1)

        @pl.when(j > 2)
        def _():
            third(j - 3)

        return carry

    lax.fori_loop(0, 15, step, 0)

    def line(o, r):
        planes = [(k, 0) for k in range(4)] + [(k, 1) for k in (3, 2, 1, 0)]
        return jnp.concatenate([acc[k, o, i, r : r + 1, :] for k, i in planes], axis=0)

    top, bottom = line(0, 0), line(0, 31)
    edge[2] = jnp.where(u == 0, bottom, top)
    remote(edge.at[2], halo.at[u, u], send.at[4], h_sem.at[4], beyond)
    halo[1 - u, u] = jnp.where(u == 0, top, bottom)
    top, bottom = line(1, 0), line(1, 31)
    edge[0] = jnp.where(u == 0, bottom, top)
    edge[1] = jnp.where(u == 0, top, bottom)
    remote(edge.at[0], halo.at[u, u], send.at[5], h_sem.at[2], partner)
    remote(edge.at[1], halo.at[1 - u, u], send.at[6], h_sem.at[3], beside)
    for k in range(4):
        for i, at in enumerate(CHUNKS[k]):
            ext[base + at] = acc[k, 1, i]

    place = lax.broadcasted_iota(jnp.int32, (32, 512), 0)

    def plane(i, carry):
        centre = ext[i + 1]
        step_x = 0.5 * (ext[i + 2] - ext[i])
        after = jnp.where(place == 31, halo[1, i // 8, pl.ds(i % 8, 1), :], pltpu.roll(centre, 31, 0))
        before = jnp.where(place == 0, halo[0, i // 8, pl.ds(i % 8, 1), :], pltpu.roll(centre, 1, 0))
        step_y = 0.5 * (after - before)
        step_z = 0.5 * (pltpu.roll(centre, 511, 1) - pltpu.roll(centre, 1, 1))
        square = step_x * step_x + step_y * step_y + step_z * step_z
        scale = -lax.rsqrt(jnp.maximum(square, 1.0))
        nrm[0, i] = (step_x * scale).astype(jnp.bfloat16)
        nrm[1, i] = (step_y * scale).astype(jnp.bfloat16)
        nrm[2, i] = (step_z * scale).astype(jnp.bfloat16)
        return carry

    wait(ext.at[pl.ds(1, 2)], e_sem.at[0])
    remote(ext.at[16], ext.at[0], send.at[7], h_sem.at[0], up)
    remote(ext.at[1], ext.at[17], send.at[8], h_sem.at[1], down)
    mine, theirs = pl.ds(8 * u, 8), pl.ds(8 * (1 - u), 8)
    level_mine = pltpu.make_async_copy(ext.at[pl.ds(base, 8)], e_ref.at[mine], store.at[0])
    level_mine.start()
    wait(halo.at[0, 0], h_sem.at[4])
    lax.fori_loop(1 + 8 * u, 7 + 8 * u, plane, 0)
    wait(halo.at[0, 0], h_sem.at[2])
    wait(halo.at[0, 0], h_sem.at[3])
    wait(ext.at[pl.ds(1, 2)], e_sem.at[1])
    lax.fori_loop(7, 9, plane, 0)
    wait(ext.at[0], h_sem.at[0])
    wait(ext.at[17], h_sem.at[1])
    plane(0, 0)
    plane(15, 0)
    normals_mine = pltpu.make_async_copy(nrm.at[:, mine], n_ref.at[:, mine], store.at[1])
    normals_mine.start()
    wait(ext.at[pl.ds(1, 2)], e_sem.at[2])
    plane(9 - 8 * u, 0)
    plane(14 - 8 * u, 0)
    wait(ext.at[pl.ds(1, 2)], e_sem.at[3])
    level_theirs = pltpu.make_async_copy(ext.at[pl.ds(9 - 8 * u, 8)], e_ref.at[theirs], store.at[2])
    level_theirs.start()
    lax.fori_loop(10 - 8 * u, 14 - 8 * u, plane, 0)
    normals_theirs = pltpu.make_async_copy(nrm.at[:, theirs], n_ref.at[:, theirs], store.at[3])
    normals_theirs.start()

    wait(out1.at[:, :, pl.ds(0, 7)], send.at[0])
    wait(a.at[:, :, pl.ds(0, 7)], send.at[1])
    wait(out2.at[:, :, :, pl.ds(0, 7)], send.at[2])
    wait(acc.at[:, 0], send.at[3])
    wait(edge.at[0], send.at[4])
    wait(edge.at[0], send.at[5])
    wait(edge.at[0], send.at[6])
    wait(ext.at[16], send.at[7])
    wait(ext.at[1], send.at[8])
    for out in (level_mine, normals_mine, level_theirs, normals_theirs):
        out.wait()


def body(coefficients):
    members, span_b, span_q, length = coefficients.shape
    data = coefficients.reshape(members, span_b * span_q, length)
    apart = pl.BlockSpec(memory_space=pl.ANY)
    f32, bf16 = jnp.float32, jnp.bfloat16
    return pl.pallas_call(
        kernel,
        out_shape=(
            jax.ShapeDtypeStruct((16, 32, 512), f32),
            jax.ShapeDtypeStruct((3, 16, 32, 512), bf16),
        ),
        in_specs=[pl.BlockSpec(memory_space=pltpu.HBM)] * 2,
        out_specs=(apart, apart),
        scratch_shapes=[
            pltpu.VMEM((3, 512, 512), bf16),
            pltpu.VMEM((6, 512, 512), bf16),
            pltpu.VMEM((3, 4, 8, 64, 128), f32),
            pltpu.VMEM((3, 4, 8, 64, 128), f32),
            pltpu.VMEM((3, 4, 8, 64, 128), f32),
            pltpu.VMEM((512, 128), bf16),
            pltpu.VMEM((512, 128), bf16),
            pltpu.VMEM((3, 4, 2, 8, 32, 128), f32),
            pltpu.VMEM((3, 4, 2, 8, 32, 128), f32),
            pltpu.VMEM((64, 512), bf16),
            pltpu.VMEM((64, 512), bf16),
            pltpu.VMEM((4, 2, 2, 32, 512), f32),
            pltpu.VMEM((18, 32, 512), f32),
            pltpu.VMEM((3, 8, 512), f32),
            pltpu.VMEM((2, 2, 8, 512), f32),
            pltpu.VMEM((3, 16, 32, 512), bf16),
            pltpu.SemaphoreType.DMA((6,)),
            pltpu.SemaphoreType.DMA((4,)),
            pltpu.SemaphoreType.DMA((9,)),
            pltpu.SemaphoreType.DMA((12,)),
            pltpu.SemaphoreType.DMA((12,)),
            pltpu.SemaphoreType.DMA((24,)),
            pltpu.SemaphoreType.DMA((4,)),
            pltpu.SemaphoreType.DMA((5,)),
        ],
        compiler_params=pltpu.CompilerParams(
            collective_id=0, has_side_effects=True, vmem_limit_bytes=VMEM_MIB * 1024 * 1024
        ),
        name="vorticity_normals",
    )(data, tables(length))


def solution(mesh):
    return jax.shard_map(
        body,
        mesh=mesh,
        in_specs=(P(None, "row", "col", None),),
        out_specs=(P("row", "col", None), P(None, "row", "col", None)),
        check_vma=False,
    )
```

time: 127 us -> 120 us (0.945)
  the two profiles are of different devices: /device:TPU:1 before, /device:TPU:8 now
where the time goes in v3:
time: 120 us
  Pallas kernels  117 us (98%)
  local copies, waits for them, and re-layouts  2.11 us (2%)
    pallas_call x1, Pallas kernels, body(): pl.pallas_call(kernel, out_shape=(jax.ShapeDtypeStruct((16, 32, 512), f32...  117 us

profile of v3, /device:TPU:8, one launch (start us, length us, event | category | flops | bytes accessed | tf_op | source)
XLA Modules:
  0.0 120.0 jit_solution(9342636113150265276)
XLA Ops:
  0.6 117.3 %vorticity_normals.1 = (f32[16,32,512]{2,1,0:T(8,128)S(1)}, bf16[3,16,32,512]{3,2,1,0:T(8,128)(2,1)S(1)}) custom-call(bf16[3,512,512]{2,1,0:T(8,128)(2,1)} %bitcast.1, bf16[6,512,512]{2,1,0:T(8,128)(2,1)} %constant.2.clone.t_hbm), custom_call_target="tpu_custom_call" | custom-call | tf_op jit(solution)/shard_map/vorticity_normals/pallas_call | solution.py:308
  117.9 1.0 copy.6
  118.9 1.1 copy.7

commit v4 on v3

--- a/solution.py
+++ b/solution.py
@@ -300,17 +300,27 @@
         out.wait()
 
 
+def write_out(level_in, normals_in, level_out, normals_out, sem):
+    pairs = ((level_in, level_out), (normals_in, normals_out))
+    copies = [pltpu.make_async_copy(a, b, sem.at[i]) for i, (a, b) in enumerate(pairs)]
+    for copy in copies:
+        copy.start()
+    for copy in copies:
+        copy.wait()
+
+
 def body(coefficients):
     members, span_b, span_q, length = coefficients.shape
     data = coefficients.reshape(members, span_b * span_q, length)
     apart = pl.BlockSpec(memory_space=pl.ANY)
     f32, bf16 = jnp.float32, jnp.bfloat16
-    return pl.pallas_call(
+    shapes = (
+        jax.ShapeDtypeStruct((16, 32, 512), f32),
+        jax.ShapeDtypeStruct((3, 16, 32, 512), bf16),
+    )
+    results = pl.pallas_call(
         kernel,
-        out_shape=(
-            jax.ShapeDtypeStruct((16, 32, 512), f32),
-            jax.ShapeDtypeStruct((3, 16, 32, 512), bf16),
-        ),
+        out_shape=shapes,
         in_specs=[pl.BlockSpec(memory_space=pltpu.HBM)] * 2,
         out_specs=(apart, apart),
         scratch_shapes=[
@@ -344,6 +354,15 @@
         ),
         name="vorticity_normals",
     )(data, tables(length))
+    return pl.pallas_call(
+        write_out,
+        out_shape=shapes,
+        in_specs=[pl.BlockSpec(memory_space=pltpu.VMEM)] * 2,
+        out_specs=(apart, apart),
+        scratch_shapes=[pltpu.SemaphoreType.DMA((2,))],
+        compiler_params=pltpu.CompilerParams(vmem_limit_bytes=8 * 1024 * 1024),
+        name="write_out",
+    )(*results)
 
 
 def solution(mesh):

time: 120 us -> 120 us (level)
  local copies, waits for them, and re-layouts: 2.11 us -> 0 us
  Pallas kernels: 117 us -> 119 us
    unnamed x2 -> x0, local copies, waits for them, and re-layouts: 2.11 us -> none
    pallas_call x1 -> x2, Pallas kernels: 117 us -> 119 us  [the longest x1 117 us: body(): pl.pallas_call(kernel, out_shape=shapes, in_specs=[pl.BlockSpec(memory_sp...]
where the time goes in v4:
time: 120 us; the launch traced here: 119 us
  Pallas kernels  119 us (99%)
    pallas_call x1, Pallas kernels, body(): pl.pallas_call(kernel, out_shape=shapes, in_specs=[pl.BlockSpec(memory_sp...  117 us

profile of v4, /device:TPU:8, one launch (start us, length us, event | category | flops | bytes accessed | tf_op | source)
XLA Modules:
  0.0 119.4 jit_solution(17230511735820545642)
XLA Ops:
  0.6 117.3 %vorticity_normals.1 = (f32[16,32,512]{2,1,0:T(8,128)S(1)}, bf16[3,16,32,512]{3,2,1,0:T(8,128)(2,1)S(1)}) custom-call(bf16[3,512,512]{2,1,0:T(8,128)(2,1)} %bitcast.1, bf16[6,512,512]{2,1,0:T(8,128)(2,1)} %constant.2.clone.t_hbm), custom_call_target="tpu_custom_call" | custom-call | tf_op jit(solution)/shard_map/vorticity_normals/pallas_call | solution.py:321
  117.9 1.5 %write_out.1 = (f32[16,32,512]{2,1,0:T(8,128)}, bf16[3,16,32,512]{3,2,1,0:T(8,128)(2,1)}) custom-call(f32[16,32,512]{2,1,0:T(8,128)S(1)} %get-tuple-element.4.level_in, bf16[3,16,32,512]{3,2,1,0:T(8,128)(2,1)S(1)} %get-tuple-element.5.normals_in), custom_call_target="tpu_custom_call" | custom-call | tf_op jit(solution)/shard_map/write_out/pallas_call | solution.py:357
